TPU v7x, 256 devices: a whole 4x4x8 slice. The times are simulated.
256 devices in a mesh: prefix: 8 (over z), feat: 32 (over y, x, core).
Axes of the slice: x: 4, y: 4, z: 8, core: 2. Of those that a mesh axis runs over, the one named last changes fastest.
Arguments:
- activations: float32 [1024, 1152], P('feat'), may hold values from -6 to 6
- enc_weight: float32 [16, 9216, 1152], P('prefix', 'feat'), may hold values from -0.1875 to 0.1875
- dec_weight: float32 [16, 9216, 1152], P('prefix', 'feat'), may hold values from -0.0625 to 0.0625
Outputs:
- enc_grad: float32 [16, 9216, 1152], P('prefix', 'feat')
- dec_grad: float32 [16, 9216, 1152], P('prefix', 'feat')
All inputs are finite; a program needn't handle non-finite values.
Results may differ from a plain program's by a relative error of at most 0.000094.
Values sent between devices are 32-bit elements; how exact they have to be, the bound alone decides.
No kernel may reach another device: no remote copies, remote signals or barrier semaphores. Data moves between devices by JAX's collectives and lax.ppermute only.
A program may use at most 128 MiB of HBM per device.

v0:
```python
import jax
import jax.numpy as jnp
from jax import lax
from jax.sharding import PartitionSpec as P

HIGHEST = lax.Precision.HIGHEST


def entering(shard, axis, combine, identity, reverse):
    count, here = (lax.axis_size(axis), lax.axis_index(axis))
    everything = lax.all_gather(shard, axis)
    start = jnp.broadcast_to(jnp.asarray(identity, shard.dtype), shard.shape)

    def step(k, before):
        at = count - 1 - k if reverse else k
        reached = at > here if reverse else at < here
        new = combine(before, everything[at])
        return jnp.where(reached, new, before)

    return lax.fori_loop(0, count, step, start)


def add_terms(earlier, later):
    return earlier + later


def chain_scan(decoded, act_rows):
    group_total = jnp.sum(decoded, axis=1)
    nothing = jnp.zeros_like(group_total)
    before = entering(group_total, "prefix", add_terms, nothing, False)
    rebuilt = before[:, None, :] + jnp.cumsum(decoded, axis=1)
    errors = rebuilt - act_rows[:, None, :]
    error_total = jnp.sum(errors, axis=1)
    beyond = entering(error_total, "prefix", add_terms, nothing, True)
    return beyond[:, None, :] + jnp.flip(jnp.cumsum(jnp.flip(errors, 1), axis=1), 1)


def per_device(activations, enc_weight, dec_weight):
    local_groups, local_feats, model_width = enc_weight.shape
    gathered = lax.all_gather(activations, "feat", axis=0, tiled=True)
    tokens = gathered.shape[0]
    pre_act = jnp.einsum("nd,gkd->gnk", gathered, enc_weight, precision=HIGHEST)
    features = jax.nn.softplus(4.0 * pre_act) / 4.0
    slopes = jax.nn.sigmoid(4.0 * pre_act)
    factor = 2.0 / tokens
    empty = jnp.zeros(enc_weight.shape, jnp.float32)
    own_rows = tokens // lax.axis_size("feat")
    feat_rows = features
    product = jnp.einsum("gnk,gkd->ngd", feat_rows, dec_weight, precision=HIGHEST)
    summed = lax.psum_scatter(
        product.reshape(lax.axis_size("feat") * own_rows, local_groups * model_width),
        "feat",
        scatter_dimension=0,
        tiled=True,
    )
    decoded = summed.reshape(summed.shape[0], local_groups, model_width)
    suffix = factor * chain_scan(decoded, activations)
    suffix_piece = lax.all_gather(suffix, "feat", axis=0, tiled=True)
    feat_rows = features
    dec_new = empty + jnp.einsum("gnk,ngd->gkd", feat_rows, suffix_piece, precision=HIGHEST)
    gate = jnp.einsum("ngd,gkd->gnk", suffix_piece, dec_weight, precision=HIGHEST) * slopes
    enc_new = empty + jnp.einsum("gnk,nd->gkd", gate, gathered, precision=HIGHEST)
    return (enc_new, dec_new)


def solution(mesh):
    in_specs = (P("feat", None), P("prefix", "feat", None), P("prefix", "feat", None))
    out_specs = (P("prefix", "feat", None), P("prefix", "feat", None))
    return jax.shard_map(
        per_device, mesh=mesh, in_specs=in_specs, out_specs=out_specs, check_vma=False
    )
```

profile of v0, /device:TPU:1, one launch (start us, length us, event | category | flops | bytes accessed | tf_op | source)
XLA Modules:
  0.0 425.4 jit_solution(15453496965193077454)
XLA Ops:
  8.0 58.4 %all-gather.7.cloned.1.call-done = f32[1024,1152]{1,0:T(8,128)} async-done(((f32[32,1152]{1,0:T(8,128)}), f32[1024,1152]{1,0:T(8,128)}) %all-gather.7.cloned.1.call-update) | async-done | bytes 4718608 | tf_op jit(solution)/shard_map/all_gather | solution.py:40
  66.4 12.5 %fusion.2 = f32[2,288,1024]{2,1,0:T(8,128)S(1)} fusion(f32[2,288,1152]{2,1,0:T(8,128)} %param.8, f32[1024,1152]{1,0:T(8,128)} %all-gather.7.cloned.1.call-done), kind=kOutput, calls=%fused_computation.6 | convolution fusion | flops 8153726976 | bytes 9732096 | tf_op jit(solution)/shard_map/nd,gkd->gnk/dot_general | solution.py:42
  78.9 1.4 copy-done.2
  80.3 19.8 %convolution_bitcast_fusion = f32[1024,2,1152]{2,0,1:T(8,128)} fusion(f32[2,288,1152]{2,1,0:T(8,128)S(1)} %copy-done, f32[2,288,1024]{2,1,0:T(8,128)S(1)} %fusion.2), kind=kOutput, calls=%fused_computation.3 | convolution fusion | flops 8158445568 | bytes 14450688 | tf_op jit(solution)/shard_map/gnk,gkd->ngd/dot_general | solution.py:49
  100.1 9.6 %copy.8 = f32[1024,2,1152]{0,2,1:T(8,128)} copy(f32[1024,2,1152]{2,0,1:T(8,128)} %convolution_bitcast_fusion) | data formatting | bytes 18874368 | tf_op jit(solution)/shard_map/gnk,gkd->ngd/transpose | solution.py:49
  109.8 9.6 %copy.13 = f32[1024,2304]{1,0:T(8,128)} copy(f32[1024,2304]{0,1:T(8,128)} %bitcast.55) | data formatting | bytes 18874368
  119.5 100.5 %reduce-scatter.4.cloned.1.call-done = f32[32,2304]{1,0:T(8,128)} async-done(((f32[1024,2304]{1,0:T(8,128)}), f32[32,2304]{1,0:T(8,128)}) %reduce-scatter.4.cloned.1.call-update) | async-done | bytes 294928
  219.9 2.3 copy.14
  222.3 1.4 reduce_sum.18
  224.7 1.6 copy.10
  226.3 33.4 %all-gather.11.cloned.1.call-done = f32[256,1152]{1,0:T(8,128)} async-done(((f32[32,1152]{1,0:T(8,128)}), f32[256,1152]{1,0:T(8,128)}) %all-gather.11.cloned.1.call-update) | async-done | bytes 1179664 | tf_op jit(solution)/shard_map/all_gather | solution.py:11
  259.7 7.8 %while.30 = (s32[]{:T(128)}, f32[32,1152]{1,0:T(8,128)S(1)}, s32[]{:T(128)}, f32[8,32,1152]{2,1,0:T(8,128)}, s32[]{:T(128)}, /*index=5*/s32[]{:T(128)}) while((s32[]{:T(128)}, f32[32,1152]{1,0:T(8,128)S(1)}, s32[]{:T(128)}, f32[8,32,1152]{2,1,0:T(8,128)}, s32[]{:T(128)}, /*index=5*/s32[]{:T(128)}) %tuple.89), condition=%wide.region_3.4_spmd.clone, body=%wide.region_2.3_spmd.clone.sunk | while | flops 110596 | bytes 442461 | solution.py:20
  261.7 1.0 add_select_fusion.4
  262.6 1.0 add_select_fusion.4
  264.6 1.0 add_select_fusion.4
  265.6 1.0 add_select_fusion.4
  268.6 12.6 %fusion.30 = f32[32,2,1152]{2,0,1:T(8,128)S(1)} fusion(f32[32,2,1152]{2,0,1:T(8,128)S(1)} %rev.7), kind=kOutput, calls=%fused_computation.36 | output fusion | flops 73728 | bytes 589824 | tf_op jit(solution)/shard_map/jit(cumsum)/reduce_window_sum | solution.py:35
  281.1 24.7 %all-gather.13.cloned.1.call-done = f32[256,1152]{1,0:T(8,128)} async-done(((f32[32,1152]{1,0:T(8,128)}), f32[256,1152]{1,0:T(8,128)}) %all-gather.13.cloned.1.call-update) | async-done | bytes 1179664 | tf_op jit(solution)/shard_map/all_gather | solution.py:11
  305.9 7.9 %while.31 = (s32[]{:T(128)}, f32[32,1152]{1,0:T(8,128)S(1)}, s32[]{:T(128)}, f32[8,32,1152]{2,1,0:T(8,128)}, s32[]{:T(128)}, /*index=5*/s32[]{:T(128)}, s32[]{:T(128)}, s32[]{:T(128)}) while((s32[]{:T(128)}, f32[32,1152]{1,0:T(8,128)S(1)}, s32[]{:T(128)}, f32[8,32,1152]{2,1,0:T(8,128)}, s32[]{:T(128)}, /*index=5*/s32[]{:T(128)}, ...), condition=%wide.region_7.8_spmd.clone, body=%wide.region_6.7_spmd.clone.sunk | while | flops 110600 | bytes 442523 | solution.py:20
  306.8 1.0 add_select_fusion.5
  314.5 64.2 %all-gather.9.cloned.1.call-done = f32[1024,2,1152]{2,0,1:T(8,128)} async-done(((f32[32,2,1152]{2,0,1:T(8,128)}), f32[1024,2,1152]{2,0,1:T(8,128)}) %all-gather.9.cloned.1.call-update) | async-done | bytes 9437200 | tf_op jit(solution)/shard_map/all_gather | solution.py:58
  378.7 13.4 %fusion.31 = f32[2,1024,288]{1,2,0:T(8,128)S(1)} fusion(f32[1024,2,1152]{2,0,1:T(8,128)} %all-gather.9.cloned.1.call-done, f32[2,288,1152]{2,1,0:T(8,128)S(1)} %copy-done), kind=kOutput, calls=%fused_computation.37 | convolution fusion | flops 8153726976 | bytes 14450688 | tf_op jit(solution)/shard_map/ngd,gkd->gnk/dot_general | solution.py:61
  392.1 12.7 %fusion.18 = f32[2,288,1152]{2,1,0:T(8,128)} fusion(f32[1024,2,1152]{2,0,1:T(8,128)S(1)} %copy-done.1, f32[2,288,1024]{2,1,0:T(8,128)S(1)} %copy-done.3), kind=kOutput, calls=%fused_computation.25 | convolution fusion | flops 8158445568 | bytes 14450688 | tf_op jit(solution)/shard_map/gnk,ngd->gkd/dot_general | solution.py:60
  404.8 13.8 %fusion = f32[2,288,1152]{2,1,0:T(8,128)} fusion(f32[1024,1152]{1,0:T(8,128)} %all-gather.7.cloned.1.call-done, f32[2,1024,288]{1,2,0:T(8,128)S(1)} %fusion.31, f32[2,288,1024]{2,1,0:T(8,128)S(1)} %copy-done.3), kind=kOutput, calls=%fused_computation.4 | convolution fusion | flops 8156676096 | bytes 12091392 | tf_op jit(solution)/shard_map/gnk,nd->gkd/dot_general | solution.py:62
  (36 shorter events, 14.0 us)
Async XLA Ops:
  7.2 73.2 %copy-start = (f32[2,288,1152]{2,1,0:T(8,128)S(1)}, f32[2,288,1152]{2,1,0:T(8,128)}, u32[]{:S(2)}) copy-start(f32[2,288,1152]{2,1,0:T(8,128)} %param.9) | copy-start | bytes 7962628
  7.2 59.2 %all-gather.7.cloned.1.call-start = ((), (), s32[]{:S(2)}) async-start(), calls=%async_computation.1 | async-start | bytes 4866048 | tf_op jit(solution)/shard_map/all_gather | solution.py:40
  7.9 212.0 %reduce-scatter.4.cloned.1.call-start = ((), (), s32[]{:S(2)}) async-start(), calls=%async_computation.5 | async-start | bytes 9732096
  78.9 1.4 copy-start.2
  119.4 140.3 %all-gather.11.cloned.1.call-start = ((), (), s32[]{:S(2)}) async-start(), calls=%async_computation.3 | async-start | bytes 1327104 | tf_op jit(solution)/shard_map/all_gather | solution.py:11
  223.7 43.8 %copy-start.4 = (f32[32,1152]{1,0:T(8,128)S(1)}, f32[32,1152]{1,0:T(8,128)}, u32[]{:S(2)}) copy-start(f32[32,1152]{1,0:T(8,128)} %param.7) | copy-start | bytes 442372
  224.6 81.2 %all-gather.13.cloned.1.call-start = ((), (), s32[]{:S(2)}) async-start(), calls=%async_computation.4 | async-start | bytes 1327104 | tf_op jit(solution)/shard_map/all_gather | solution.py:11
  268.5 110.2 %all-gather.9.cloned.1.call-start = ((), (), s32[]{:S(2)}) async-start(), calls=%async_computation.2 | async-start | bytes 9732096 | tf_op jit(solution)/shard_map/all_gather | solution.py:58
  378.7 13.4 %copy-start.1 = (f32[1024,2,1152]{2,0,1:T(8,128)S(1)}, f32[1024,2,1152]{2,0,1:T(8,128)}, u32[]{:S(2)}) copy-start(f32[1024,2,1152]{2,0,1:T(8,128)} %all-gather.9.cloned.1.call-done) | copy-start | bytes 28311556
  378.7 13.4 %copy-start.3 = (f32[2,288,1024]{2,1,0:T(8,128)S(1)}, f32[2,288,1024]{2,1,0:T(8,128)}, u32[]{:S(2)}) copy-start(f32[2,288,1024]{2,1,0:T(8,128)} %copy-done.2) | copy-start | bytes 7077892
Sparse Core Ops, SparseCore 0:
  10.5 55.8 all-gather.6
  119.5 100.3 reduce-scatter.3
  224.7 34.9 all-gather.10
  268.6 37.2 all-gather.12
  314.6 64.0 all-gather.8
where the time goes:
time: 430 us; the launch traced here: 425 us
  waiting for transfers between devices  282 us (66%)
  matrix products  72.2 us (17%)
  other arithmetic  30.9 us (7%)
  local copies, waits for them, and re-layouts  25.5 us (6%)
  between operations  14.1 us (3%)
    unnamed x6, waiting for transfers between devices  101 us
    all_gather x1, waiting for transfers between devices, per_device(): suffix_piece = lax.all_gather(suffix, 'feat', axis=0, tiled=True)  64.2 us
    all_gather x1, waiting for transfers between devices, per_device(): gathered = lax.all_gather(activations, 'feat', axis=0, tiled=True)  58.4 us
    all_gather x2, waiting for transfers between devices, entering(): everything = lax.all_gather(shard, axis)  58.2 us
    dot_general x1, matrix products, per_device(): jnp.einsum('gnk,gkd->ngd', feat_rows, dec_weight, precision=HIGHEST)  19.8 us
    select_n x16, other arithmetic, step(): return jnp.where(reached, new, before)  15.3 us
    unnamed x13, local copies, waits for them, and re-layouts  14.3 us
    dot_general x1, matrix products, per_device(): jnp.einsum('gnk,nd->gkd', gate, gathered, precision=HIGHEST)  13.8 us
  transfers between devices with their start and end apart: 5, of which 5 were waited for; matrix products, arithmetic and copies ran while one was open for 3% of the time, Pallas kernels for 0%

commit v1 on v0

--- a/solution.py
+++ b/solution.py
@@ -37,7 +37,10 @@
 
 def per_device(activations, enc_weight, dec_weight):
     local_groups, local_feats, model_width = enc_weight.shape
-    gathered = lax.all_gather(activations, "feat", axis=0, tiled=True)
+    u_next = jax.lax.axis_size("feat")
+    val2 = jnp.stack(u_next * [activations], axis=0)
+    all_values = jax.lax.all_to_all(val2, axis_name="feat", split_axis=0, concat_axis=0)
+    gathered = jnp.concatenate(all_values, axis=0)
     tokens = gathered.shape[0]
     pre_act = jnp.einsum("nd,gkd->gnk", gathered, enc_weight, precision=HIGHEST)
     features = jax.nn.softplus(4.0 * pre_act) / 4.0

time: 430 us -> 438 us (1.019)
  blocking collectives: 0 us -> 65 us
  waiting for transfers between devices: 282 us -> 235 us
  other arithmetic: 30.9 us -> 18.9 us
    all_to_all x0 -> x1, blocking collectives: none -> 65 us  [per_device(): jax.lax.all_to_all(val2, axis_name='feat', split_axis=0, concat_axis=0)]
    all_gather x1 -> x0, waiting for transfers between devices: 58.4 us -> none  [per_device(): gathered = lax.all_gather(activations, 'feat', axis=0, tiled=True)]
    another operation x1, other arithmetic: 12.6 us -> 0.54 us  [chain_scan(): jnp.cumsum(jnp.flip(errors, 1), axis=1)]
    all_gather x2, waiting for transfers between devices: 58.2 us -> 70.2 us  [entering(): everything = lax.all_gather(shard, axis)]
    unnamed x6 -> x5, waiting for transfers between devices: 101 us -> 101 us
    unnamed x13 -> x21, local copies, waits for them, and re-layouts: 14.3 us -> 14.3 us
  transfers between devices with their start and end apart: 5 -> 4, of which waited for: 5 -> 4; matrix products, arithmetic and copies ran while one was open for 3% -> 1% of each run, Pallas kernels for 0% -> 0%
where the time goes in v1:
time: 438 us; the launch traced here: 429 us
  waiting for transfers between devices  235 us (54%)
  matrix products  68.7 us (16%)
  blocking collectives  65 us (15%)
  local copies, waits for them, and re-layouts  27.1 us (6%)
  other arithmetic  18.9 us (4%)
  between operations  14.1 us (3%)
    unnamed x5, waiting for transfers between devices  101 us
    all_gather x2, waiting for transfers between devices, entering(): everything = lax.all_gather(shard, axis)  70.2 us
    all_to_all x1, blocking collectives, per_device(): jax.lax.all_to_all(val2, axis_name='feat', split_axis=0, concat_axis=0)  65 us
    all_gather x1, waiting for transfers between devices, per_device(): suffix_piece = lax.all_gather(suffix, 'feat', axis=0, tiled=True)  64.2 us
    dot_general x1, matrix products, per_device(): jnp.einsum('gnk,gkd->ngd', feat_rows, dec_weight, precision=HIGHEST)  19.6 us
    select_n x16, other arithmetic, step(): return jnp.where(reached, new, before)  15.3 us
    unnamed x21, local copies, waits for them, and re-layouts  14.3 us
    dot_general x1, matrix products, per_device(): jnp.einsum('gnk,nd->gkd', gate, gathered, precision=HIGHEST)  13.8 us
  transfers between devices with their start and end apart: 4, of which 4 were waited for; matrix products, arithmetic and copies ran while one was open for 1% of the time, Pallas kernels for 0%

profile of v1, /device:TPU:1, one launch (start us, length us, event | category | flops | bytes accessed | tf_op | source)
XLA Modules:
  0.0 429.4 jit_solution(10685869489608518564)
XLA Ops:
  7.2 1.6 stack.2
  8.8 65.0 %all_to_all.5 = f32[32,32,1152]{2,1,0:T(8,128)S(1)} all-to-all(f32[32,32,1152]{2,1,0:T(8,128)S(1)} %stack.2), channel_id=1, replica_groups=mesh['prefix'=8,'feat'=32] {'feat'}, dimensions={0} | all-to-all | bytes 9437184 | tf_op jit(solution)/shard_map/all_to_all | solution.py:42
  73.8 9.5 %fusion.28 = f32[2,288,1024]{2,1,0:T(8,128)S(1)} fusion(f32[2,288,1152]{2,1,0:T(8,128)S(1)} %copy-done.4, f32[1024,1152,1]{1,0,2:T(8,128)S(1)} %bitcast.58), kind=kOutput, calls=%fused_computation.34 | convolution fusion | flops 8153726976 | bytes 9732096 | tf_op jit(solution)/shard_map/nd,gkd->gnk/dot_general | solution.py:45
  83.4 1.4 copy-done.1
  84.8 19.6 %convolution_bitcast_fusion = f32[1024,2,1152]{2,0,1:T(8,128)} fusion(f32[2,288,1152]{2,1,0:T(8,128)S(1)} %copy-done, f32[2,288,1024]{2,1,0:T(8,128)S(1)} %fusion.28), kind=kOutput, calls=%fused_computation.3 | convolution fusion | flops 8158445568 | bytes 14450688 | tf_op jit(solution)/shard_map/gnk,gkd->ngd/dot_general | solution.py:52
  104.3 9.6 %copy.8 = f32[1024,2,1152]{0,2,1:T(8,128)} copy(f32[1024,2,1152]{2,0,1:T(8,128)} %convolution_bitcast_fusion) | data formatting | bytes 18874368 | tf_op jit(solution)/shard_map/gnk,gkd->ngd/transpose | solution.py:52
  114.0 9.6 %copy.13 = f32[1024,2304]{1,0:T(8,128)} copy(f32[1024,2304]{0,1:T(8,128)} %bitcast.57) | data formatting | bytes 18874368
  123.7 100.5 %reduce-scatter.4.cloned.1.call-done = f32[32,2304]{1,0:T(8,128)} async-done(((f32[1024,2304]{1,0:T(8,128)}), f32[32,2304]{1,0:T(8,128)}) %reduce-scatter.4.cloned.1.call-update) | async-done | bytes 294928
  224.2 2.3 copy.14
  226.5 1.4 reduce_sum.18
  228.9 1.6 copy.10
  230.5 33.4 %all-gather.8.cloned.1.call-done = f32[256,1152]{1,0:T(8,128)} async-done(((f32[32,1152]{1,0:T(8,128)}), f32[256,1152]{1,0:T(8,128)}) %all-gather.8.cloned.1.call-update) | async-done | bytes 1179664 | tf_op jit(solution)/shard_map/all_gather | solution.py:11
  264.0 7.8 %while.30 = (s32[]{:T(128)}, f32[32,1152]{1,0:T(8,128)S(1)}, s32[]{:T(128)}, f32[8,32,1152]{2,1,0:T(8,128)}, s32[]{:T(128)}, /*index=5*/s32[]{:T(128)}) while((s32[]{:T(128)}, f32[32,1152]{1,0:T(8,128)S(1)}, s32[]{:T(128)}, f32[8,32,1152]{2,1,0:T(8,128)}, s32[]{:T(128)}, /*index=5*/s32[]{:T(128)}) %tuple.87), condition=%wide.region_3.4_spmd.clone, body=%wide.region_2.3_spmd.clone.sunk | while | flops 110596 | bytes 442461 | solution.py:20
  264.9 1.0 add_select_fusion.4
  265.9 1.0 add_select_fusion.4
  267.9 1.0 add_select_fusion.4
  268.9 1.0 add_select_fusion.4
  270.8 1.0 add_select_fusion.4
  273.4 36.8 %all-gather.10.cloned.1.call-done = f32[256,1152]{1,0:T(8,128)} async-done(((f32[32,1152]{1,0:T(8,128)}), f32[256,1152]{1,0:T(8,128)}) %all-gather.10.cloned.1.call-update) | async-done | bytes 1179664 | tf_op jit(solution)/shard_map/all_gather | solution.py:11
  310.1 7.9 %while.31 = (s32[]{:T(128)}, f32[32,1152]{1,0:T(8,128)S(1)}, s32[]{:T(128)}, f32[8,32,1152]{2,1,0:T(8,128)}, s32[]{:T(128)}, /*index=5*/s32[]{:T(128)}, s32[]{:T(128)}, s32[]{:T(128)}) while((s32[]{:T(128)}, f32[32,1152]{1,0:T(8,128)S(1)}, s32[]{:T(128)}, f32[8,32,1152]{2,1,0:T(8,128)}, s32[]{:T(128)}, /*index=5*/s32[]{:T(128)}, ...), condition=%wide.region_7.8_spmd.clone, body=%wide.region_6.7_spmd.clone.sunk | while | flops 110600 | bytes 442523 | solution.py:20
  318.7 64.2 %all-gather.6.cloned.1.call-done = f32[1024,2,1152]{2,0,1:T(8,128)} async-done(((f32[32,2,1152]{2,0,1:T(8,128)}), f32[1024,2,1152]{2,0,1:T(8,128)}) %all-gather.6.cloned.1.call-update) | async-done | bytes 9437200 | tf_op jit(solution)/shard_map/all_gather | solution.py:61
  382.9 13.0 %fusion.29 = f32[2,1024,288]{1,2,0:T(8,128)S(1)} fusion(f32[1024,2,1152]{2,0,1:T(8,128)} %all-gather.6.cloned.1.call-done, f32[2,288,1152]{2,1,0:T(8,128)S(1)} %copy-done), kind=kOutput, calls=%fused_computation.35 | convolution fusion | flops 8153726976 | bytes 14450688 | tf_op jit(solution)/shard_map/ngd,gkd->gnk/dot_general | solution.py:64
  396.0 13.8 %fusion.5 = f32[2,288,1152]{2,1,0:T(8,128)} fusion(f32[1024,1152,1]{1,0,2:T(8,128)} %bitcast.59, f32[2,1024,288]{1,2,0:T(8,128)S(1)} %fusion.29, f32[2,288,1024]{2,1,0:T(8,128)S(1)} %copy-done.2), kind=kOutput, calls=%fused_computation.13 | convolution fusion | flops 8156676096 | bytes 12091392 | tf_op jit(solution)/shard_map/gnk,nd->gkd/dot_general | solution.py:65
  409.8 12.9 %fusion.15 = f32[2,288,1152]{2,1,0:T(8,128)} fusion(f32[1024,2,1152]{2,0,1:T(8,128)S(1)} %bitcast.56, f32[2,288,1024]{2,1,0:T(8,128)S(1)} %copy-done.2), kind=kOutput, calls=%fused_computation.22 | convolution fusion | flops 8158445568 | bytes 14450688 | tf_op jit(solution)/shard_map/gnk,ngd->gkd/dot_general | solution.py:63
  (44 shorter events, 13.9 us)
Async XLA Ops:
  7.2 77.6 %copy-start = (f32[2,288,1152]{2,1,0:T(8,128)S(1)}, f32[2,288,1152]{2,1,0:T(8,128)}, u32[]{:S(2)}) copy-start(f32[2,288,1152]{2,1,0:T(8,128)} %param.9) | copy-start | bytes 7962628
  7.2 217.0 %reduce-scatter.4.cloned.1.call-start = ((), (), s32[]{:S(2)}) async-start(), calls=%async_computation.5 | async-start | bytes 9732096
  8.8 65.0 %copy-start.4 = (f32[2,288,1152]{2,1,0:T(8,128)S(1)}, f32[2,288,1152]{2,1,0:T(8,128)}, u32[]{:S(2)}) copy-start(f32[2,288,1152]{2,1,0:T(8,128)} %param.8) | copy-start | bytes 7962628
  73.8 9.5 %copy-start.3 = (f32[32,32,1152]{2,1,0:T(8,128)}, f32[32,32,1152]{2,1,0:T(8,128)S(1)}, u32[]{:S(2)}) copy-start(f32[32,32,1152]{2,1,0:T(8,128)S(1)} %all_to_all.5) | copy-start | bytes 14155780
  83.4 1.4 copy-start.1
  123.6 140.3 %all-gather.8.cloned.1.call-start = ((), (), s32[]{:S(2)}) async-start(), calls=%async_computation.3 | async-start | bytes 1327104 | tf_op jit(solution)/shard_map/all_gather | solution.py:11
  227.9 43.8 %copy-start.5 = (f32[32,1152]{1,0:T(8,128)S(1)}, f32[32,1152]{1,0:T(8,128)}, u32[]{:S(2)}) copy-start(f32[32,1152]{1,0:T(8,128)} %param.7) | copy-start | bytes 442372
  228.9 81.2 %all-gather.10.cloned.1.call-start = ((), (), s32[]{:S(2)}) async-start(), calls=%async_computation.4 | async-start | bytes 1327104 | tf_op jit(solution)/shard_map/all_gather | solution.py:11
  272.7 110.2 %all-gather.6.cloned.1.call-start = ((), (), s32[]{:S(2)}) async-start(), calls=%async_computation.2 | async-start | bytes 9732096 | tf_op jit(solution)/shard_map/all_gather | solution.py:61
  382.9 13.0 %copy-start.2 = (f32[2,288,1024]{2,1,0:T(8,128)S(1)}, f32[2,288,1024]{2,1,0:T(8,128)}, u32[]{:S(2)}) copy-start(f32[2,288,1024]{2,1,0:T(8,128)} %copy-done.1) | copy-start | bytes 7077892
  382.9 26.9 %slice-start = ((s8[9437184]{0:T(1024)(128)(4,1)}), s8[4194304]{0:T(1024)(128)(4,1)S(1)}, s32[]{:S(2)}) async-start(s8[9437184]{0:T(1024)(128)(4,1)} %bitcast.55), calls=%async_computation.6 | async-start | bytes 8388608
  382.9 26.9 %slice-start.1 = ((s8[9437184]{0:T(1024)(128)(4,1)}), s8[1048576]{0:T(1024)(128)(4,1)S(1)}, s32[]{:S(2)}) async-start(s8[9437184]{0:T(1024)(128)(4,1)} %bitcast.55), calls=%async_computation.7 | async-start | bytes 2097152
  396.0 13.8 %slice-start.2 = ((s8[9437184]{0:T(1024)(128)(4,1)}), s8[4194304]{0:T(1024)(128)(4,1)S(1)}, s32[]{:S(2)}) async-start(s8[9437184]{0:T(1024)(128)(4,1)} %bitcast.55), calls=%async_computation.8 | async-start | bytes 8388608
Sparse Core Ops, SparseCore 0:
  123.7 100.3 reduce-scatter.3
  229.0 34.9 all-gather.7
  272.8 37.2 all-gather.9
  318.9 64.0 all-gather.5
